TPU v7x, 256 devices: a whole 4x4x8 slice. The times are simulated.
256 devices in a mesh: dp: 32 (over y, z), vocab: 8 (over x, core).
Axes of the slice: x: 4, y: 4, z: 8, core: 2. Of those that a mesh axis runs over, the one named last changes fastest.
Arguments:
- hidden: bfloat16 [24576, 2048], P('dp', 'vocab')
- gain: bfloat16 [2048], replicated, may hold values from 0.5 to 1.5
- head: bfloat16 [2048, 32000], P('dp', 'vocab')
- target_ids: int32 [24576], P('dp'), may hold values from 0 to 31999
- seq_lens: int32 [64], replicated, may hold values from 64 to 704, as said below
- seq_owner: int32 [64], replicated, may hold values from 0 to 31, as said below
Outputs:
- logprob: float32 [24576], P('dp')
- entropy: float32 [24576], P('dp')
Inputs may be any that keep to these rules, and one draw needn't show every extreme that they name: `seq_lens`: the lengths of the sequences owned by one dp index sum to at most 768; in every draw the sequences of some dp index sum to exactly 768. `seq_owner`: every dp index owns exactly 2 sequences.
All inputs are finite; a program needn't handle non-finite values.
Results may differ from a plain program's by a relative error of at most 0.0075.
Values may be sent and summed in bfloat16 or wider, within the bound.
A program may use at most 64 MiB of HBM per device.

v0:
```python
import jax
import jax.numpy as jnp
from jax import lax
from jax.sharding import PartitionSpec as P

EPS = 1e-05


def chunk_bounds(breadth, parts):
    step = -(-breadth // parts)
    step = -(-step // 128) * 128
    bounds = []
    start = 0
    while start < breadth:
        stop = min(start + step, breadth)
        bounds.append((start, stop))
        start = stop
    return bounds


def chunk_stats(normed, columns, local_id, start):
    logits = jnp.dot(normed, columns, preferred_element_type=jnp.float32)
    top = jnp.max(logits, axis=1)
    expo = jnp.exp(logits - top[:, None])
    total = jnp.sum(expo, axis=1)
    weighted = jnp.sum(expo * logits, axis=1)
    ids = start + lax.broadcasted_iota(jnp.int32, logits.shape, 1)
    picked = jnp.sum(jnp.where(ids == local_id[:, None], logits, 0.0), axis=1)
    return (top, total, weighted, picked)


def local(hidden, gain, head, target_ids, seq_lens, seq_owner):
    groups = lax.axis_size("dp")
    position = lax.axis_index("dp")
    slice_index = lax.axis_index("vocab")
    slots = hidden.shape[0]
    breadth = head.shape[1]
    owners = jnp.arange(groups, dtype=jnp.int32)
    loads = jnp.sum(jnp.where(seq_owner[:, None] == owners[None, :], seq_lens[:, None], 0), axis=0)
    own_live = jnp.arange(slots, dtype=jnp.int32) < loads[position]
    features = lax.all_gather(hidden, "vocab", axis=1, tiled=True)
    wide = features.astype(jnp.float32)
    normed = (
        wide
        * lax.rsqrt(jnp.mean(wide * wide, axis=1, keepdims=True) + EPS)
        * gain.astype(jnp.float32)
    ).astype(jnp.bfloat16)
    local_id = target_ids - slice_index * breadth
    parts = []
    for start, stop in chunk_bounds(breadth, 4):
        columns = lax.all_gather(head[:, start:stop], "dp", axis=0, tiled=True)
        parts.append(chunk_stats(normed, columns, local_id, start))
    tops = jnp.stack([p[0] for p in parts])
    top_local = jnp.max(tops, axis=0)
    scale = jnp.exp(tops - top_local[None, :])
    total_local = jnp.sum(jnp.stack([p[1] for p in parts]) * scale, axis=0)
    weighted_local = jnp.sum(jnp.stack([p[2] for p in parts]) * scale, axis=0)
    picked_local = jnp.sum(jnp.stack([p[3] for p in parts]), axis=0)
    top = lax.pmax(top_local, "vocab")
    factor = jnp.exp(top_local - top)
    total, weighted, picked = lax.psum(
        (total_local * factor, weighted_local * factor, picked_local), "vocab"
    )
    lse = top + jnp.log(total)
    logprob = picked - lse
    entropy = lse - weighted / total
    return (jnp.where(own_live, logprob, 0.0), jnp.where(own_live, entropy, 0.0))


def solution(mesh):
    return jax.shard_map(
        local,
        mesh=mesh,
        in_specs=(P("dp", "vocab"), P(), P("dp", "vocab"), P("dp"), P(), P()),
        out_specs=(P("dp"), P("dp")),
        check_vma=False,
    )
```

profile of v0, /device:TPU:32, one launch (start us, length us, event | category | flops | bytes accessed | tf_op | source)
XLA Modules:
  0.0 432.0 jit_solution(7421292452426967437)
XLA Ops:
  7.2 0.0 all-gather.6.cloned.1.call-start
  7.2 0.7 all-gather.6.cloned.1.call-update
  7.9 0.0 all-gather.14.cloned.1.call-start
  7.9 1.6 slice.15
  9.5 0.0 all-gather.14.cloned.1.call-update
  9.5 0.0 all-gather.8.cloned.1.call-start
  9.6 1.8 fusion.20
  11.4 0.0 all-gather.8.cloned.1.call-update
  11.4 0.0 all-gather.10.cloned.1.call-start
  11.5 0.5 all-gather.10.cloned.1.call-update
  12.0 0.0 all-gather.12.cloned.1.call-start
  12.0 0.5 all-gather.12.cloned.1.call-update
  12.6 0.7 convert_element_type.10
  13.3 0.8 select_reduce_fusion.4
  14.1 0.7 dynamic_slice.3
  14.7 0.7 broadcast_subtract_fusion
  15.4 31.2 %all-gather.6.cloned.1.call-done = bf16[768,2048]{1,0:T(8,128)(2,1)} async-done(((bf16[768,256]{1,0:T(8,128)(2,1)}), bf16[768,2048]{1,0:T(8,128)(2,1)}) %all-gather.6.cloned.1.call-update) | async-done | bytes 3145744 | tf_op jit(solution)/shard_map/all_gather | solution.py:41
  46.6 2.7 fusion
  49.4 82.9 %all-gather.14.cloned.1.call-done = bf16[2048,928]{1,0:T(8,128)(2,1)} async-done(((bf16[64,928]{1,0:T(8,128)(2,1)}), bf16[2048,928]{1,0:T(8,128)(2,1)}) %all-gather.14.cloned.1.call-update) | async-done | bytes 3801104 | tf_op jit(solution)/shard_map/all_gather | solution.py:51
  132.3 5.9 %fusion.21 = (f32[768]{0:T(1024)S(1)}, f32[768,928]{0,1:T(8,128)S(1)}) fusion(bf16[2048,928]{1,0:T(8,128)(2,1)} %all-gather.14.cloned.1.call-done, bf16[768,2048]{1,0:T(8,128)(2,1)S(1)} %copy-done.1, f32[2048]{0:T(1024)S(1)} %convert_element_type.10, f32[768]{0:T(1024)S(1)} %add_rsqrt_fusion), kind=kOutput, calls=%fused_computation.49 | convolution fusion | flops 2926238976 | bytes 9811968 | tf_op jit(solution)/shard_map/dot_general | solution.py:22
  138.2 0.9 multiply_reduce_fusion.3
  139.0 74.9 %all-gather.8.cloned.1.call-done = bf16[2048,1024]{1,0:T(8,128)(2,1)} async-done(((bf16[64,1024]{1,0:T(8,128)(2,1)}), bf16[2048,1024]{1,0:T(8,128)(2,1)}) %all-gather.8.cloned.1.call-update) | async-done | bytes 4194320 | tf_op jit(solution)/shard_map/all_gather | solution.py:51
  214.0 6.4 %fusion.24 = (f32[768]{0:T(1024)S(1)}, f32[768,1024]{1,0:T(8,128)S(1)}) fusion(bf16[2048,1024]{1,0:T(8,128)(2,1)} %all-gather.8.cloned.1.call-done, bf16[768,2048]{1,0:T(8,128)(2,1)} %all-gather.6.cloned.1.call-done, f32[2048]{0:T(1024)S(1)} %convert_element_type.10, f32[768]{0:T(1024)S(1)} %add_rsqrt_fusion), kind=kOutput, calls=%fused_computation.52 | convolution fusion | flops 3228302592 | bytes 10500096 | tf_op jit(solution)/shard_map/dot_general | solution.py:22
  220.4 75.1 %all-gather.10.cloned.1.call-done = bf16[2048,1024]{1,0:T(8,128)(2,1)} async-done(((bf16[64,1024]{1,0:T(8,128)(2,1)}), bf16[2048,1024]{1,0:T(8,128)(2,1)}) %all-gather.10.cloned.1.call-update) | async-done | bytes 4194320 | tf_op jit(solution)/shard_map/all_gather | solution.py:51
  295.5 8.4 %fusion.22 = (f32[768]{0:T(1024)S(1)}, f32[768,1024]{1,0:T(8,128)}) fusion(bf16[2048,1024]{1,0:T(8,128)(2,1)} %all-gather.10.cloned.1.call-done, bf16[768,2048]{1,0:T(8,128)(2,1)} %all-gather.6.cloned.1.call-done, f32[2048]{0:T(1024)S(1)} %convert_element_type.10, f32[768]{0:T(1024)S(1)} %add_rsqrt_fusion), kind=kOutput, calls=%fused_computation.50 | convolution fusion | flops 3228302592 | bytes 10500096 | tf_op jit(solution)/shard_map/dot_general | solution.py:22
  303.8 73.2 %all-gather.12.cloned.1.call-done = bf16[2048,1024]{1,0:T(8,128)(2,1)} async-done(((bf16[64,1024]{1,0:T(8,128)(2,1)}), bf16[2048,1024]{1,0:T(8,128)(2,1)}) %all-gather.12.cloned.1.call-update) | async-done | bytes 4194320 | tf_op jit(solution)/shard_map/all_gather | solution.py:51
  377.0 6.6 %fusion.23 = (f32[768]{0:T(1024)S(1)}, f32[768,1024]{1,0:T(8,128)S(1)}) fusion(bf16[2048,1024]{1,0:T(8,128)(2,1)} %all-gather.12.cloned.1.call-done, bf16[768,2048]{1,0:T(8,128)(2,1)} %all-gather.6.cloned.1.call-done, f32[2048]{0:T(1024)S(1)} %convert_element_type.10, f32[768]{0:T(1024)S(1)} %add_rsqrt_fusion), kind=kOutput, calls=%fused_computation.51 | convolution fusion | flops 3228302592 | bytes 10500096 | tf_op jit(solution)/shard_map/dot_general | solution.py:22
  383.6 4.4 %multiply_reduce_fusion.1 = (f32[768]{0:T(1024)S(1)}, f32[768]{0:T(1024)S(1)}, f32[768]{0:T(1024)S(1)}, f32[768]{0:T(1024)S(1)}, f32[768]{0:T(1024)S(1)}, /*inde...) fusion(f32[768,1024]{1,0:T(8,128)S(1)} %copy-done, f32[768]{0:T(1024)S(1)} %get-tuple-element.34, ...), kind=kLoop, calls=%fused_computation.6 | loop fusion | flops 16508160 | bytes 9485312 | tf_op jit(solution)/shard_map/reduce_sum | solution.py:26
  388.1 12.4 %pmax.7 = f32[768]{0:T(1024)S(1)} all-reduce(f32[768]{0:T(1024)S(1)} %maximum_maximum_fusion), channel_id=1, replica_groups=mesh['dp'=32,'vocab'=8] {'vocab'}, use_global_device_ids=true, to_apply=%region_11.12 | all-reduce | flops 768 | bytes 6144 | tf_op jit(solution)/shard_map/pmax | solution.py:59
  400.5 0.1 fusion.9
  400.6 23.6 %all-reduce = (f32[768]{0:T(1024)S(1)}, f32[768]{0:T(1024)S(1)}, f32[768]{0:T(1024)S(1)}) all-reduce(f32[768]{0:T(1024)S(1)} %add_add_fusion, f32[768]{0:T(1024)S(1)} %get-tuple-element.25, f32[768]{0:T(1024)S(1)} %get-tuple-element.24), channel_id=1, replica_groups=mesh['dp'=32,'vocab'=8] {'vocab'}, use_global_device_ids=true, to_apply=%region_6.7 | all-reduce | flops 2304 | bytes 18432 | tf_op jit(solution)/shard_map/psum | solution.py:61
  424.2 1.3 subtract_select_fusion
  (22 shorter events, 0.1 us)
Async XLA Ops:
  7.2 39.5 %all-gather.6.cloned.1.call-start = ((), (), s32[]{:S(2)}) async-start(), calls=%async_computation | async-start | bytes 3538944 | tf_op jit(solution)/shard_map/all_gather | solution.py:41
  7.9 124.4 %all-gather.14.cloned.1.call-start = ((), (), s32[]{:S(2)}) async-start(), calls=%async_computation.4 | async-start | bytes 4325376 | tf_op jit(solution)/shard_map/all_gather | solution.py:51
  9.5 204.4 %all-gather.8.cloned.1.call-start = ((), (), s32[]{:S(2)}) async-start(), calls=%async_computation.1 | async-start | bytes 4325376 | tf_op jit(solution)/shard_map/all_gather | solution.py:51
  11.4 284.1 %all-gather.10.cloned.1.call-start = ((), (), s32[]{:S(2)}) async-start(), calls=%async_computation.2 | async-start | bytes 4325376 | tf_op jit(solution)/shard_map/all_gather | solution.py:51
  12.0 365.0 %all-gather.12.cloned.1.call-start = ((), (), s32[]{:S(2)}) async-start(), calls=%async_computation.3 | async-start | bytes 4325376 | tf_op jit(solution)/shard_map/all_gather | solution.py:51
  46.6 85.6 %copy-start.1 = (bf16[768,2048]{1,0:T(8,128)(2,1)S(1)}, bf16[768,2048]{1,0:T(8,128)(2,1)}, u32[]{:S(2)}) copy-start(bf16[768,2048]{1,0:T(8,128)(2,1)} %all-gather.6.cloned.1.call-done) | copy-start | bytes 9437188
  377.0 6.6 %copy-start = (f32[768,1024]{1,0:T(8,128)S(1)}, f32[768,1024]{1,0:T(8,128)}, u32[]{:S(2)}) copy-start(f32[768,1024]{1,0:T(8,128)} %get-tuple-element.35) | copy-start | bytes 9437188
Sparse Core Ops, SparseCore 0:
  9.8 36.7 all-gather.5
  49.2 83.0 all-gather.13
  134.9 79.0 all-gather.7
  216.4 79.0 all-gather.9
  297.9 79.0 all-gather.11
where the time goes:
time: 432 us
  waiting for transfers between devices  339 us (78%)
  blocking collectives  36 us (8%)
  matrix products  27.2 us (6%)
  between operations  13.9 us (3%)
  other arithmetic  11.6 us (3%)
    all_gather x4, waiting for transfers between devices, local(): columns = lax.all_gather(head[:, start:stop], 'dp', axis=0, tiled=True)  306 us
    all_gather x1, waiting for transfers between devices, local(): features = lax.all_gather(hidden, 'vocab', axis=1, tiled=True)  31.2 us
    dot_general x4, matrix products, chunk_stats(): logits = jnp.dot(normed, columns, preferred_element_type=jnp.float32)  27.2 us
    psum x1, blocking collectives, local(): lax.psum((total_local * factor, weighted_local * factor, picked_local), '...  23.6 us
    pmax x1, blocking collectives, local(): top = lax.pmax(top_local, 'vocab')  12.4 us
  transfers between devices with their start and end apart: 5, of which 5 were waited for; matrix products, arithmetic and copies ran while one was open for 7% of the time, Pallas kernels for 0%

commit v1 on v0

--- a/solution.py
+++ b/solution.py
@@ -48,7 +48,9 @@
     local_id = target_ids - slice_index * breadth
     parts = []
     for start, stop in chunk_bounds(breadth, 4):
-        columns = lax.all_gather(head[:, start:stop], "dp", axis=0, tiled=True)
+        shard = head[:, start:stop]
+        copies = jnp.concatenate([shard] * lax.axis_size("dp"), axis=0)
+        columns = lax.all_to_all(copies, "dp", 0, 0, tiled=True)
         parts.append(chunk_stats(normed, columns, local_id, start))
     tops = jnp.stack([p[0] for p in parts])
     top_local = jnp.max(tops, axis=0)

time: 432 us -> 494 us (1.14)
  local copies, waits for them, and re-layouts: 4.11 us -> 78.8 us
  waiting for transfers between devices: 339 us -> 292 us
  starting transfers between devices: 0.2 us -> 32.3 us
    all_gather x4 -> x0, waiting for transfers between devices: 306 us -> none  [local(): columns = lax.all_gather(head[:, start:stop], 'dp', axis=0, tiled=True)]
    all_to_all x0 -> x4, waiting for transfers between devices: none -> 291 us  [local(): columns = lax.all_to_all(copies, 'dp', 0, 0, tiled=True)]
    unnamed x4 -> x139, local copies, waits for them, and re-layouts: 0.01 us -> 76 us
    all_to_all x0 -> x4, starting transfers between devices: none -> 32.3 us  [local(): columns = lax.all_to_all(copies, 'dp', 0, 0, tiled=True)]
    all_gather x1, waiting for transfers between devices: 31.2 us -> 0.02 us  [local(): features = lax.all_gather(hidden, 'vocab', axis=1, tiled=True)]
  transfers between devices with their start and end apart: 5 -> 5, of which waited for: 5 -> 4; matrix products, arithmetic and copies ran while one was open for 7% -> 18% of each run, Pallas kernels for 0% -> 0%
where the time goes in v1:
time: 494 us; the launch traced here: 493 us
  waiting for transfers between devices  292 us (59%)
  local copies, waits for them, and re-layouts  78.8 us (16%)
  blocking collectives  38.3 us (8%)
  starting transfers between devices  32.3 us (7%)
  matrix products  28.1 us (6%)
  between operations  14.5 us (3%)
  other arithmetic  9.21 us (2%)
    all_to_all x4, waiting for transfers between devices, local(): columns = lax.all_to_all(copies, 'dp', 0, 0, tiled=True)  291 us
    unnamed x139, local copies, waits for them, and re-layouts  76 us
    all_to_all x4, starting transfers between devices, local(): columns = lax.all_to_all(copies, 'dp', 0, 0, tiled=True)  32.3 us
    dot_general x4, matrix products, chunk_stats(): logits = jnp.dot(normed, columns, preferred_element_type=jnp.float32)  28.1 us
    psum x1, blocking collectives, local(): lax.psum((total_local * factor, weighted_local * factor, picked_local), '...  23.6 us
    pmax x1, blocking collectives, local(): top = lax.pmax(top_local, 'vocab')  14.7 us
  transfers between devices with their start and end apart: 5, of which 4 were waited for; matrix products, arithmetic and copies ran while one was open for 18% of the time, Pallas kernels for 0%

profile of v1, /device:TPU:32, one launch (start us, length us, event | category | flops | bytes accessed | tf_op | source)
XLA Modules:
  0.0 493.5 jit_solution(12105957242149085369)
XLA Ops:
  7.2 1.0 constant_dynamic-update-slice_fusion.127
  8.2 0.9 constant_dynamic-update-slice_fusion.126
  9.1 0.9 constant_dynamic-update-slice_fusion.125
  10.0 0.9 constant_dynamic-update-slice_fusion.124
  10.9 0.9 constant_dynamic-update-slice_fusion.123
  11.8 0.9 constant_dynamic-update-slice_fusion.122
  12.8 0.9 constant_dynamic-update-slice_fusion.121
  13.7 0.9 constant_dynamic-update-slice_fusion.120
  14.6 0.9 constant_dynamic-update-slice_fusion.119
  15.5 0.9 constant_dynamic-update-slice_fusion.118
  16.4 0.9 constant_dynamic-update-slice_fusion.117
  17.4 0.9 constant_dynamic-update-slice_fusion.116
  18.3 0.9 constant_dynamic-update-slice_fusion.115
  19.2 0.9 constant_dynamic-update-slice_fusion.114
  22.3 2.0 copy-done.1
  24.2 11.4 %all-to-all-start.3 = ((bf16[32,64,928]{2,1,0:T(8,128)(2,1)}), bf16[32,64,928]{2,1,0:T(8,128)(2,1)}, u32[]{:S(2)}, u32[]{:S(2)}) async-start(bf16[32,64,928]{2,1,0:T(8,128)(2,1)} %bitcast.14), calls=%async_computation.3 | async-start | bytes 8388608 | tf_op jit(solution)/shard_map/all_to_all | solution.py:53
  73.3 57.9 %all-to-all-done.3 = bf16[32,64,928]{2,1,0:T(8,128)(2,1)} async-done(((bf16[32,64,928]{2,1,0:T(8,128)(2,1)}), bf16[32,64,928]{2,1,0:T(8,128)(2,1)}, u32[]{:S(2)}, u32[]{:S(2)}) %all-to-all-start.3) | async-done | bytes 3801120 | tf_op jit(solution)/shard_map/all_to_all | solution.py:53
  131.2 6.7 %all-to-all-start.1 = ((bf16[32,64,1024]{2,1,0:T(8,128)(2,1)}), bf16[32,64,1024]{2,1,0:T(8,128)(2,1)}, u32[]{:S(2)}, u32[]{:S(2)}) async-start(bf16[32,64,1024]{2,1,0:T(8,128)(2,1)} %bitcast.3), calls=%async_computation.1 | async-start | bytes 8388608 | tf_op jit(solution)/shard_map/all_to_all | solution.py:53
  161.6 71.4 %all-to-all-done.1 = bf16[32,64,1024]{2,1,0:T(8,128)(2,1)} async-done(((bf16[32,64,1024]{2,1,0:T(8,128)(2,1)}), bf16[32,64,1024]{2,1,0:T(8,128)(2,1)}, u32[]{:S(2)}, u32[]{:S(2)}) %all-to-all-start.1) | async-done | bytes 4194336 | tf_op jit(solution)/shard_map/all_to_all | solution.py:53
  233.0 7.3 %all-to-all-start.2 = ((bf16[32,64,1024]{2,1,0:T(8,128)(2,1)}), bf16[32,64,1024]{2,1,0:T(8,128)(2,1)}, u32[]{:S(2)}, u32[]{:S(2)}) async-start(bf16[32,64,1024]{2,1,0:T(8,128)(2,1)} %bitcast.13), calls=%async_computation.2 | async-start | bytes 8388608 | tf_op jit(solution)/shard_map/all_to_all | solution.py:53
  241.1 94.5 %all-to-all-done.2 = bf16[32,64,1024]{2,1,0:T(8,128)(2,1)} async-done(((bf16[32,64,1024]{2,1,0:T(8,128)(2,1)}), bf16[32,64,1024]{2,1,0:T(8,128)(2,1)}, u32[]{:S(2)}, u32[]{:S(2)}) %all-to-all-start.2) | async-done | bytes 4194336 | tf_op jit(solution)/shard_map/all_to_all | solution.py:53
  335.6 6.8 %all-to-all-start = ((bf16[32,64,1024]{2,1,0:T(8,128)(2,1)}), bf16[32,64,1024]{2,1,0:T(8,128)(2,1)}, u32[]{:S(2)}, u32[]{:S(2)}) async-start(bf16[32,64,1024]{2,1,0:T(8,128)(2,1)} %bitcast.1), calls=%async_computation | async-start | bytes 8388608 | tf_op jit(solution)/shard_map/all_to_all | solution.py:53
  343.2 2.6 fusion
  345.8 6.8 %fusion.20 = (f32[768]{0:T(1024)S(1)}, f32[768,928]{0,1:T(8,128)S(1)}) fusion(bf16[2048,928]{1,0:T(8,128)(2,1)} %bitcast.8, bf16[768,2048]{1,0:T(8,128)(2,1)} %all-gather.2.cloned.1.call-done, f32[2048]{0:T(1024)S(1)} %convert_element_type.10, f32[768]{0:T(1024)S(1)} %add_rsqrt_fusion), kind=kOutput, calls=%fused_computation.176 | convolution fusion | flops 2926238976 | bytes 9811968 | tf_op jit(solution)/shard_map/dot_general | solution.py:22
  353.6 7.4 %fusion.22 = (f32[768]{0:T(1024)S(1)}, f32[768,1024]{1,0:T(8,128)}) fusion(bf16[2048,1024]{1,0:T(8,128)(2,1)} %bitcast.6, bf16[768,2048]{1,0:T(8,128)(2,1)S(1)} %copy-done.4, f32[2048]{0:T(1024)S(1)} %convert_element_type.10, f32[768]{0:T(1024)S(1)} %add_rsqrt_fusion), kind=kOutput, calls=%fused_computation.178 | convolution fusion | flops 3228302592 | bytes 10500096 | tf_op jit(solution)/shard_map/dot_general | solution.py:22
  360.9 7.4 %fusion.21 = (f32[768]{0:T(1024)S(1)}, f32[768,1024]{1,0:T(8,128)}) fusion(bf16[2048,1024]{1,0:T(8,128)(2,1)} %bitcast.4, bf16[768,2048]{1,0:T(8,128)(2,1)S(1)} %copy-done.4, f32[2048]{0:T(1024)S(1)} %convert_element_type.10, f32[768]{0:T(1024)S(1)} %add_rsqrt_fusion), kind=kOutput, calls=%fused_computation.177 | convolution fusion | flops 3228302592 | bytes 10500096 | tf_op jit(solution)/shard_map/dot_general | solution.py:22
  368.3 67.7 %all-to-all-done = bf16[32,64,1024]{2,1,0:T(8,128)(2,1)} async-done(((bf16[32,64,1024]{2,1,0:T(8,128)(2,1)}), bf16[32,64,1024]{2,1,0:T(8,128)(2,1)}, u32[]{:S(2)}, u32[]{:S(2)}) %all-to-all-start) | async-done | bytes 4194336 | tf_op jit(solution)/shard_map/all_to_all | solution.py:53
  436.0 6.6 %fusion.23 = (f32[768]{0:T(1024)S(1)}, f32[768,1024]{1,0:T(8,128)S(1)}) fusion(bf16[2048,1024]{1,0:T(8,128)(2,1)} %bitcast.2, bf16[768,2048]{1,0:T(8,128)(2,1)} %all-gather.2.cloned.1.call-done, f32[2048]{0:T(1024)S(1)} %convert_element_type.10, f32[768]{0:T(1024)S(1)} %add_rsqrt_fusion), kind=kOutput, calls=%fused_computation.179 | convolution fusion | flops 3228302592 | bytes 10500096 | tf_op jit(solution)/shard_map/dot_general | solution.py:22
  442.6 4.4 multiply_reduce_fusion.1
  447.0 14.7 %pmax.7 = f32[768]{0:T(1024)S(1)} all-reduce(f32[768]{0:T(1024)S(1)} %maximum_maximum_fusion), channel_id=1, replica_groups=mesh['dp'=32,'vocab'=8] {'vocab'}, use_global_device_ids=true, to_apply=%region_11.12 | all-reduce | flops 768 | bytes 6144 | tf_op jit(solution)/shard_map/pmax | solution.py:61
  461.9 23.6 %all-reduce = (f32[768]{0:T(1024)S(1)}, f32[768]{0:T(1024)S(1)}, f32[768]{0:T(1024)S(1)}) all-reduce(f32[768]{0:T(1024)S(1)} %add_add_fusion, f32[768]{0:T(1024)S(1)} %get-tuple-element.27, f32[768]{0:T(1024)S(1)} %get-tuple-element.26), channel_id=1, replica_groups=mesh['dp'=32,'vocab'=8] {'vocab'}, use_global_device_ids=true, to_apply=%region_6.7 | all-reduce | flops 2304 | bytes 18432 | tf_op jit(solution)/shard_map/psum | solution.py:63
  485.4 1.2 subtract_select_fusion
  (155 shorter events, 65.8 us)
Async XLA Ops:
  7.2 14.8 %copy-start = (bf16[64,4000]{1,0:T(8,128)(2,1)S(1)}, bf16[64,4000]{1,0:T(8,128)(2,1)}, u32[]{:S(2)}) copy-start(bf16[64,4000]{1,0:T(8,128)(2,1)} %param.8) | copy-start | bytes 1536004
  22.3 2.0 copy-start.1
  24.2 106.9 %all-to-all-start.3 = ((bf16[32,64,928]{2,1,0:T(8,128)(2,1)}), bf16[32,64,928]{2,1,0:T(8,128)(2,1)}, u32[]{:S(2)}, u32[]{:S(2)}) async-start(bf16[32,64,928]{2,1,0:T(8,128)(2,1)} %bitcast.14), calls=%async_computation.3 | async-start | bytes 8388608 | tf_op jit(solution)/shard_map/all_to_all | solution.py:53
  131.2 101.8 %all-to-all-start.1 = ((bf16[32,64,1024]{2,1,0:T(8,128)(2,1)}), bf16[32,64,1024]{2,1,0:T(8,128)(2,1)}, u32[]{:S(2)}, u32[]{:S(2)}) async-start(bf16[32,64,1024]{2,1,0:T(8,128)(2,1)} %bitcast.3), calls=%async_computation.1 | async-start | bytes 8388608 | tf_op jit(solution)/shard_map/all_to_all | solution.py:53
  233.0 102.6 %all-to-all-start.2 = ((bf16[32,64,1024]{2,1,0:T(8,128)(2,1)}), bf16[32,64,1024]{2,1,0:T(8,128)(2,1)}, u32[]{:S(2)}, u32[]{:S(2)}) async-start(bf16[32,64,1024]{2,1,0:T(8,128)(2,1)} %bitcast.13), calls=%async_computation.2 | async-start | bytes 8388608 | tf_op jit(solution)/shard_map/all_to_all | solution.py:53
  240.3 102.9 %all-gather.2.cloned.1.call-start = ((), (), s32[]{:S(2)}) async-start(), calls=%async_computation.4 | async-start | bytes 3538944 | tf_op jit(solution)/shard_map/all_gather | solution.py:41
  335.6 6.8 %copy-start.5 = (bf16[2048]{0:T(1024)(128)(2,1)S(1)}, bf16[2048]{0:T(1024)(128)(2,1)}, u32[]{:S(2)}) copy-start(bf16[2048]{0:T(1024)(128)(2,1)} %param.7) | copy-start | bytes 12292
  335.6 6.9 %copy-start.7 = (s32[64]{0:T(128)S(1)}, s32[64]{0:T(128)}, u32[]{:S(2)}) copy-start(s32[64]{0:T(128)} %param.10) | copy-start | bytes 772
  335.6 6.9 %copy-start.8 = (s32[64]{0:T(128)S(1)}, s32[64]{0:T(128)}, u32[]{:S(2)}) copy-start(s32[64]{0:T(128)} %param.11) | copy-start | bytes 772
  335.6 7.6 %copy-start.6 = (s32[768]{0:T(1024)S(1)}, s32[768]{0:T(1024)}, u32[]{:S(2)}) copy-start(s32[768]{0:T(1024)} %param.9) | copy-start | bytes 9220
  335.6 100.4 %all-to-all-start = ((bf16[32,64,1024]{2,1,0:T(8,128)(2,1)}), bf16[32,64,1024]{2,1,0:T(8,128)(2,1)}, u32[]{:S(2)}, u32[]{:S(2)}) async-start(bf16[32,64,1024]{2,1,0:T(8,128)(2,1)} %bitcast.1), calls=%async_computation | async-start | bytes 8388608 | tf_op jit(solution)/shard_map/all_to_all | solution.py:53
  345.8 7.7 %copy-start.4 = (bf16[768,2048]{1,0:T(8,128)(2,1)S(1)}, bf16[768,2048]{1,0:T(8,128)(2,1)}, u32[]{:S(2)}) copy-start(bf16[768,2048]{1,0:T(8,128)(2,1)} %all-gather.2.cloned.1.call-done) | copy-start | bytes 9437188
  436.0 6.6 %copy-start.2 = (f32[768,1024]{1,0:T(8,128)S(1)}, f32[768,1024]{1,0:T(8,128)}, u32[]{:S(2)}) copy-start(f32[768,1024]{1,0:T(8,128)} %get-tuple-element.39) | copy-start | bytes 9437188
  436.0 6.6 %copy-start.3 = (f32[768,1024]{1,0:T(8,128)S(1)}, f32[768,1024]{1,0:T(8,128)}, u32[]{:S(2)}) copy-start(f32[768,1024]{1,0:T(8,128)} %get-tuple-element.37) | copy-start | bytes 9437188
Sparse Core Ops, SparseCore 0:
  243.0 35.1 all-gather.1
